TPU v7x, 32 devices: a whole 2x2x4 slice. The times are simulated.
32 devices in a mesh: seq: 8 (over z, y), feat: 4 (over x, core).
Axes of the slice: x: 2, y: 2, z: 4, core: 2. Of those that a mesh axis runs over, the one named last changes fastest.
Arguments:
- activations_in: bfloat16 [6144, 512], P('seq', 'feat'), may hold values from -6 to 6
- cotangent: bfloat16 [6144, 512], P('seq', 'feat'), may hold values from -6 to 6
- seq_start: int32 [16], P('seq'), may hold values from 0 to 768, as said below
- seq_length: int32 [16], P('seq'), may hold values from 0 to 768, as said below
- input_matrix: float32 [2, 512, 768], P(None, 'feat'), may hold values from -0.25 to 0.25
- output_matrix: float32 [2, 1536, 512], P(None, None, 'feat'), may hold values from -1.25 to 1.25
- gate_matrix: float32 [2, 512, 512], P(None, None, 'feat'), may hold values from -0.25 to 0.25
- feature_vectors: float32 [2, 4, 512], P(None, None, 'feat'), may hold values from 0.1 to 1.9
- state_vectors: float32 [2, 3, 384], replicated, may hold values from -20 to 20, as said below
- velocity_input: float32 [2, 512, 768], P(None, 'feat'), may hold values from -6 to 6
- velocity_output: float32 [2, 1536, 512], P(None, None, 'feat'), may hold values from -6 to 6
- velocity_gate: float32 [2, 512, 512], P(None, None, 'feat'), may hold values from -6 to 6
- velocity_feature: float32 [2, 4, 512], P(None, None, 'feat'), may hold values from -6 to 6
- velocity_state: float32 [2, 3, 384], replicated, may hold values from -6 to 6
- average_input: float32 [2, 512, 768], P(None, 'feat'), may hold values from -0.25 to 0.25
- average_output: float32 [2, 1536, 512], P(None, None, 'feat'), may hold values from -1.25 to 1.25
- average_gate: float32 [2, 512, 512], P(None, None, 'feat'), may hold values from -0.25 to 0.25
- average_feature: float32 [2, 4, 512], P(None, None, 'feat'), may hold values from 0.1 to 1.9
- average_state: float32 [2, 3, 384], replicated, may hold values from -3 to 1
Outputs:
- activations_out: float32 [6144, 512], P('seq', 'feat')
- input_gradient: float32 [6144, 512], P('seq', 'feat')
- gradient_input: float32 [2, 512, 768], P(None, 'feat')
- gradient_output: float32 [2, 1536, 512], P(None, None, 'feat')
- gradient_gate: float32 [2, 512, 512], P(None, None, 'feat')
- gradient_feature: float32 [2, 4, 512], P(None, None, 'feat')
- gradient_state: float32 [2, 3, 384], replicated
- updated_input: float32 [2, 512, 768], P(None, 'feat')
- updated_output: float32 [2, 1536, 512], P(None, None, 'feat')
- updated_gate: float32 [2, 512, 512], P(None, None, 'feat')
- updated_feature: float32 [2, 4, 512], P(None, None, 'feat')
- state_change: float32 [2, 3, 384], replicated
- momentum_input: float32 [2, 512, 768], P(None, 'feat')
- momentum_output: float32 [2, 1536, 512], P(None, None, 'feat')
- momentum_gate: float32 [2, 512, 512], P(None, None, 'feat')
- momentum_feature: float32 [2, 4, 512], P(None, None, 'feat')
- momentum_state: float32 [2, 3, 384], replicated
- smoothed_input: float32 [2, 512, 768], P(None, 'feat')
- smoothed_output: float32 [2, 1536, 512], P(None, None, 'feat')
- smoothed_gate: float32 [2, 512, 512], P(None, None, 'feat')
- smoothed_feature: float32 [2, 4, 512], P(None, None, 'feat')
- smoothed_state: float32 [2, 3, 384], replicated
Inputs may be any that keep to these rules, and one draw needn't show every extreme that they name: `seq_length`: sequences of a device lie in its own buffer, ordered and without intersection; one device holds a single sequence of 768 tokens and an empty slot, every other device two sequences of 192 to 384 tokens. `seq_start`: positions within a device's buffer; a slot of length zero starts at 768. `state_vectors`: rows hold log(-Re Lambda), Im Lambda and the log timestep.
All inputs are finite; a program needn't handle non-finite values.
Results may differ from a plain program's by a relative error of at most 0.012.
The roundings to bfloat16 on the way count: a program that leaves them out, or rounds other values in their place, can miss the bound.
Values may be sent and summed in bfloat16 or wider, within the bound.
A program may use at most 448 MiB of HBM per device.

v0:
```python
import math
import jax
import jax.numpy as jnp
from jax import lax
from jax.sharding import PartitionSpec as P

epsilon = 1e-05
momentum = 0.9
smoothing = 0.5
slow_rate = 0.02
main_rate = 0.05
weight_decay = 0.1


def smooth(value):
    return jax.nn.gelu(value, approximate=False)


def combine(earlier, later):
    mult_real = later[0] * earlier[0] - later[1] * earlier[1]
    mult_imag = later[0] * earlier[1] + later[1] * earlier[0]
    add_real = later[0] * earlier[2] - later[1] * earlier[3] + later[2]
    add_imag = later[0] * earlier[3] + later[1] * earlier[2] + later[3]
    return (mult_real, mult_imag, add_real, add_imag)


def masks_of(starts, lengths, count):
    position = jnp.arange(count, dtype=jnp.int32)[:, None]
    begin = starts[None, :]
    finish = begin + lengths[None, :]
    inside = (position >= begin) & (position < finish)
    alive = jnp.any(inside, 1)
    opening = jnp.any(inside & (position == begin), 1)
    closing = jnp.any(inside & (position == finish - 1), 1)
    return (
        alive.astype(jnp.float32),
        (alive & ~opening).astype(jnp.float32),
        (alive & ~closing).astype(jnp.float32),
    )


def prefix(current, backward):
    length = current[2].shape[0]
    offset = 1
    while offset < length:

        def shifted(value):
            filler = jnp.zeros((offset,) + value.shape[1:], value.dtype)
            if backward:
                return jnp.concatenate([value[offset:], filler], 0)
            return jnp.concatenate([filler, value[: length - offset]], 0)

        earlier = tuple((shifted(value) for value in current))
        current = combine(earlier, current)
        offset = offset * 2
    return current


def scan_states(drive, state_row, alive, carry_prev, carry_next):
    width = state_row.shape[1]
    rate = -jnp.exp(state_row[0])
    frequency = state_row[1]
    timestep = jnp.exp(state_row[2])
    decay = jnp.exp(rate * timestep)
    angle = frequency * timestep
    pole_real = decay * jnp.cos(angle)
    pole_imag = decay * jnp.sin(angle)
    denom = rate * rate + frequency * frequency
    factor_real = ((pole_real - 1.0) * rate + pole_imag * frequency) / denom
    factor_imag = (pole_imag * rate - (pole_real - 1.0) * frequency) / denom
    drive_real = drive[:, :width]
    drive_imag = drive[:, width:]
    input_real = (drive_real * factor_real - drive_imag * factor_imag) * alive[:, None]
    input_imag = (drive_real * factor_imag + drive_imag * factor_real) * alive[:, None]
    ahead = prefix(
        (carry_prev[:, None] * pole_real, carry_prev[:, None] * pole_imag, input_real, input_imag),
        False,
    )
    behind = prefix(
        (carry_next[:, None] * pole_real, carry_next[:, None] * pole_imag, input_real, input_imag),
        True,
    )
    return jnp.concatenate([ahead[2], ahead[3], behind[2], behind[3]], 1)


def update(weight, gradient, velocity, average, rate, decay):
    adjusted = gradient + decay * weight
    velocity_new = momentum * velocity + adjusted
    change = -rate * (adjusted + momentum * velocity_new)
    weight_new = weight + change
    average_new = smoothing * average + (1.0 - smoothing) * weight_new
    return (weight_new, velocity_new, average_new, change)


def contract_rows(left, right):
    return lax.dot_general(
        left, right, (((0,), (0,)), ((), ())), preferred_element_type=jnp.float32
    )


def contract_cols(left, right):
    return lax.dot_general(
        left, right, (((1,), (1,)), ((), ())), preferred_element_type=jnp.float32
    )


def moments(stream):
    whole = lax.all_gather(stream, "feat", axis=1, tiled=True)
    center = jnp.mean(whole, 1, keepdims=True)
    spread = whole - center
    variance = jnp.mean(spread * spread, 1, keepdims=True)
    return (center, lax.rsqrt(variance + epsilon))


def back_moments(unit_grad, unit):
    spread_grad, crossed = (
        lax.all_gather(unit_grad, "feat", axis=1, tiled=True),
        lax.all_gather(unit_grad * unit, "feat", axis=1, tiled=True),
    )
    return (jnp.mean(spread_grad, 1, keepdims=True), jnp.mean(crossed, 1, keepdims=True))


def state_forward(normed_low, in_low, state_row, masks):
    partial_drive = jnp.dot(normed_low, in_low, preferred_element_type=jnp.float32)
    drive = lax.psum(partial_drive, "feat")
    states = scan_states(drive, state_row, masks[0], masks[1], masks[2])
    return (drive, states.astype(jnp.bfloat16))


def state_backward(drive, state_row, masks, mixed_low, out_low):

    def scanned(drive_in, rows_in):
        return scan_states(drive_in, rows_in, masks[0], masks[1], masks[2])

    partial_states = contract_cols(mixed_low, out_low)
    states_grad = lax.psum(partial_states, "feat")
    unused, pull = jax.vjp(scanned, drive, state_row)
    drive_grad, row_grad = pull(states_grad)
    return (drive_grad.astype(jnp.bfloat16), row_grad)


def body(
    activations_in,
    cotangent,
    seq_start,
    seq_length,
    input_matrix,
    output_matrix,
    gate_matrix,
    feature_vectors,
    state_vectors,
    velocity_input,
    velocity_output,
    velocity_gate,
    velocity_feature,
    velocity_state,
    average_input,
    average_output,
    average_gate,
    average_feature,
    average_state,
):
    count = activations_in.shape[0]
    layers = input_matrix.shape[0]
    masks = masks_of(seq_start, seq_length, count)
    stream = activations_in.astype(jnp.float32)
    saved = []
    for layer in range(layers):
        in_low = input_matrix[layer].astype(jnp.bfloat16)
        out_low = output_matrix[layer].astype(jnp.bfloat16)
        gate_low = gate_matrix[layer].astype(jnp.bfloat16)
        feature_row = feature_vectors[layer]
        center, scale = moments(stream)
        unit = (stream - center) * scale
        normed = unit * feature_row[0] + feature_row[1]
        normed_low = normed.astype(jnp.bfloat16)
        drive, states_low = state_forward(normed_low, in_low, state_vectors[layer], masks)
        mixed = (
            jnp.dot(states_low, out_low, preferred_element_type=jnp.float32)
            + feature_row[2] * normed
        )
        act = smooth(mixed)
        act_all = lax.all_gather(act.astype(jnp.bfloat16), "feat", axis=1, tiled=True)
        pre = jnp.dot(act_all, gate_low, preferred_element_type=jnp.float32) + feature_row[3]
        saved.append((scale, unit, normed, normed_low, drive, states_low, mixed, act, act_all, pre))
        stream = stream + act * jax.nn.sigmoid(pre)
    grad = cotangent.astype(jnp.float32) * masks[0][:, None]
    layer_grads = [None] * layers
    for layer in reversed(range(layers)):
        scale, unit, normed, normed_low, drive, states_low, mixed, act, act_all, pre = saved[layer]
        in_low = input_matrix[layer].astype(jnp.bfloat16)
        out_low = output_matrix[layer].astype(jnp.bfloat16)
        gate_low = gate_matrix[layer].astype(jnp.bfloat16)
        feature_row = feature_vectors[layer]
        gate = jax.nn.sigmoid(pre)
        pre_grad = (grad * act * gate * (1.0 - gate)).astype(jnp.bfloat16)
        gate_grad = contract_rows(act_all, pre_grad)
        gate_bias_grad = jnp.sum(pre_grad.astype(jnp.float32), 0)
        act_grad = grad * gate + lax.psum_scatter(
            contract_cols(pre_grad, gate_low), "feat", scatter_dimension=1, tiled=True
        )
        mixed_grad = jax.vjp(smooth, mixed)[1](act_grad)[0]
        skip_grad = jnp.sum(mixed_grad * normed, 0)
        mixed_low = mixed_grad.astype(jnp.bfloat16)
        out_grad = contract_rows(states_low, mixed_low)
        drive_low, row_grad = state_backward(drive, state_vectors[layer], masks, mixed_low, out_low)
        in_grad = contract_rows(normed_low, drive_low)
        normed_grad = mixed_grad * feature_row[2] + contract_cols(drive_low, in_low)
        gain_grad = jnp.sum(normed_grad * unit, 0)
        bias_grad = jnp.sum(normed_grad, 0)
        unit_grad = normed_grad * feature_row[0]
        first_mean, second_mean = back_moments(unit_grad, unit)
        grad = grad + scale * (unit_grad - first_mean - unit * second_mean)
        feature_grad = jnp.stack([gain_grad, bias_grad, skip_grad, gate_bias_grad])
        layer_grads[layer] = (in_grad, out_grad, gate_grad, feature_grad, row_grad)
    stacked_in = jnp.stack([entry[0] for entry in layer_grads])
    stacked_out = jnp.stack([entry[1] for entry in layer_grads])
    stacked_gate = jnp.stack([entry[2] for entry in layer_grads])
    stacked_feature = jnp.stack([entry[3] for entry in layer_grads])
    stacked_state = jnp.stack([entry[4] for entry in layer_grads])
    summed = lax.psum(
        (stacked_in, stacked_out, stacked_gate, stacked_feature, stacked_state), "seq"
    )
    factor = 1.0 / math.sqrt(count * lax.axis_size("seq"))
    grad_in = summed[0] * factor
    grad_out = summed[1] * factor
    grad_gate = summed[2] * factor
    grad_feature = summed[3] * factor
    grad_state = summed[4] * factor
    new_in = update(input_matrix, grad_in, velocity_input, average_input, slow_rate, 0.0)
    new_out = update(output_matrix, grad_out, velocity_output, average_output, slow_rate, 0.0)
    new_gate = update(gate_matrix, grad_gate, velocity_gate, average_gate, main_rate, weight_decay)
    new_feature = update(
        feature_vectors, grad_feature, velocity_feature, average_feature, main_rate, weight_decay
    )
    new_state = update(state_vectors, grad_state, velocity_state, average_state, slow_rate, 0.0)
    return (
        stream,
        grad,
        grad_in,
        grad_out,
        grad_gate,
        grad_feature,
        grad_state,
        new_in[0],
        new_out[0],
        new_gate[0],
        new_feature[0],
        new_state[3],
        new_in[1],
        new_out[1],
        new_gate[1],
        new_feature[1],
        new_state[1],
        new_in[2],
        new_out[2],
        new_gate[2],
        new_feature[2],
        new_state[2],
    )


def solution(mesh):
    return jax.shard_map(
        body,
        mesh=mesh,
        in_specs=(
            P("seq", "feat"),
            P("seq", "feat"),
            P("seq"),
            P("seq"),
            P(None, "feat", None),
            P(None, None, "feat"),
            P(None, None, "feat"),
            P(None, None, "feat"),
            P(),
            P(None, "feat", None),
            P(None, None, "feat"),
            P(None, None, "feat"),
            P(None, None, "feat"),
            P(),
            P(None, "feat", None),
            P(None, None, "feat"),
            P(None, None, "feat"),
            P(None, None, "feat"),
            P(),
        ),
        out_specs=(
            P("seq", "feat"),
            P("seq", "feat"),
            P(None, "feat", None),
            P(None, None, "feat"),
            P(None, None, "feat"),
            P(None, None, "feat"),
            P(),
            P(None, "feat", None),
            P(None, None, "feat"),
            P(None, None, "feat"),
            P(None, None, "feat"),
            P(),
            P(None, "feat", None),
            P(None, None, "feat"),
            P(None, None, "feat"),
            P(None, None, "feat"),
            P(),
            P(None, "feat", None),
            P(None, None, "feat"),
            P(None, None, "feat"),
            P(None, None, "feat"),
            P(),
        ),
        check_vma=False,
    )
```

profile of v0, /device:TPU:0, one launch (start us, length us, event | category | flops | bytes accessed | tf_op | source)
XLA Modules:
  0.0 1222.3 jit_solution(16966885579422786372)
XLA Ops:
  10.5 22.2 %all-gather.7.cloned.1.call-done = f32[768,512]{1,0:T(8,128)} async-done(((f32[768,128]{1,0:T(8,128)}), f32[768,512]{1,0:T(8,128)}) %all-gather.7.cloned.1.call-update) | async-done | bytes 1572880 | tf_op jit(solution)/shard_map/all_gather | solution.py:108
  43.4 52.2 %all-reduce.322.cloned.1.call-done = f32[768,768]{1,0:T(8,128)} async-done(((f32[768,768]{1,0:T(8,128)}), f32[768,768]{1,0:T(8,128)}) %all-reduce.322.cloned.1.call-update) | async-done | bytes 2359312 | tf_op jit(solution)/shard_map/psum | solution.py:125
  154.0 8.2 all_gather.25
  164.5 20.4 %all-gather.9.cloned.1.call-done = f32[768,512]{1,0:T(8,128)} async-done(((f32[768,128]{1,0:T(8,128)}), f32[768,512]{1,0:T(8,128)}) %all-gather.9.cloned.1.call-update) | async-done | bytes 1572880 | tf_op jit(solution)/shard_map/all_gather | solution.py:108
  192.1 55.7 %all-reduce.324.cloned.1.call-done = f32[768,768]{1,0:T(8,128)} async-done(((f32[768,768]{1,0:T(8,128)}), f32[768,768]{1,0:T(8,128)}) %all-reduce.324.cloned.1.call-update) | async-done | bytes 2359312 | tf_op jit(solution)/shard_map/psum | solution.py:125
  306.8 8.2 all_gather.27
  320.8 28.8 %reduce-scatter.3.cloned.1.call-done = f32[768,128]{1,0:T(8,128)} async-done(((f32[768,512]{1,0:T(8,128)}), f32[768,128]{1,0:T(8,128)}) %reduce-scatter.3.cloned.1.call-update) | async-done | bytes 393232 | tf_op jit(solution)/shard_map/reduce_scatter | solution.py:199
  352.9 3.9 fusion.341
  357.1 93.9 %all-reduce.326.cloned.1.call-done = f32[768,1536]{1,0:T(8,128)} async-done(((f32[768,1536]{1,0:T(8,128)}), f32[768,1536]{1,0:T(8,128)}) %all-reduce.326.cloned.1.call-update) | async-done | bytes 4718608 | tf_op jit(solution)/shard_map/psum | solution.py:136
  451.0 5.1 fusion.478
  461.9 5.8 fusion.447
  467.7 3.6 fusion.502
  494.6 4.0 fusion.445
  506.1 3.8 fusion.444
  517.8 4.0 fusion.432
  528.8 4.2 fusion.431
  541.2 3.4 fusion.443
  550.6 3.4 fusion.442
  562.2 3.8 fusion.430
  574.6 3.8 fusion.429
  586.3 4.0 fusion.441
  599.9 4.0 fusion.440
  611.9 3.9 fusion.439
  622.0 3.7 multiply_reduce_fusion.3
  629.3 3.4 fusion.428
  645.8 3.5 multiply_reduce_fusion.2
  659.7 19.4 %all-gather.13.cloned.1.call-done = f32[768,512]{1,0:T(8,128)} async-done(((f32[768,128]{1,0:T(8,128)}), f32[768,512]{1,0:T(8,128)}) %all-gather.13.cloned.1.call-update) | async-done | bytes 1572880 | tf_op jit(solution)/shard_map/all_gather | solution.py:118
  680.7 20.4 %all-gather.11.cloned.1.call-done = f32[768,512]{1,0:T(8,128)} async-done(((f32[768,128]{1,0:T(8,128)}), f32[768,512]{1,0:T(8,128)}) %all-gather.11.cloned.1.call-update) | async-done | bytes 1572880 | tf_op jit(solution)/shard_map/all_gather | solution.py:117
  707.7 28.3 %reduce-scatter.5.cloned.1.call-done = f32[768,128]{1,0:T(8,128)} async-done(((f32[768,512]{1,0:T(8,128)}), f32[768,128]{1,0:T(8,128)}) %reduce-scatter.5.cloned.1.call-update) | async-done | bytes 393232 | tf_op jit(solution)/shard_map/reduce_scatter | solution.py:199
  737.9 3.9 fusion.340
  742.3 93.7 %all-reduce.328.cloned.1.call-done = f32[768,1536]{1,0:T(8,128)} async-done(((f32[768,1536]{1,0:T(8,128)}), f32[768,1536]{1,0:T(8,128)}) %all-reduce.328.cloned.1.call-update) | async-done | bytes 4718608 | tf_op jit(solution)/shard_map/psum | solution.py:136
  836.0 4.8 fusion.477
  846.5 5.0 fusion.423
  851.6 3.6 fusion.486
  867.6 3.4 fusion.409
  885.6 3.4 fusion.420
  894.9 3.6 fusion.408
  904.8 3.9 fusion.407
  916.5 3.8 fusion.419
  928.0 3.8 fusion.418
  940.1 3.8 fusion.406
  952.5 3.9 fusion.405
  964.5 4.0 fusion.417
  978.2 4.0 fusion.416
  990.1 3.9 fusion.415
  1006.9 3.4 fusion.404
  1049.8 37.1 %all-reduce.314 = (f32[2,4,128]{2,1,0:T(4,128)S(1)}, f32[2,3,384]{2,1,0:T(4,128)S(1)}) all-reduce(f32[2,4,128]{2,1,0:T(4,128)S(1)} %pad_maximum_fusion.10, f32[2,3,384]{2,1,0:T(4,128)S(1)} %pad_maximum_fusion.9), channel_id=1, replica_groups=mesh['seq'=8,'feat'=4] {'seq'}, use_global_device_ids=true, to_apply=%region_28.0 | all-reduce | flops 3328 | bytes 26624 | tf_op jit(solution)/shard_map/psum | solution.py:221
  1095.4 110.1 %all-reduce.330.cloned.1.call-done = (f32[2,128,768]{2,1,0:T(8,128)}, f32[2,1536,128]{2,1,0:T(8,128)}, f32[2,512,128]{2,1,0:T(8,128)}) async-done(((f32[2,128,768]{2,1,0:T(8,128)}, f32[2,1536,128]{2,1,0:T(8,128)}, f32[2,512,128]{2,1,0:T(8,128)}), (f32[2,128,768]{2,1,0:T(8,128)}, f32[2,1536,128]{2,1,0:T(8,128)}, f32[2,512,128]{2,1,0:T(8,128)})) %all-reduce.330.cloned.1.call-update) | async-done | bytes 2883600 | tf_op jit(solution)/shard_map/psum | solution.py:221
  (1613 shorter events, 469.7 us)
Async XLA Ops:
  7.2 25.5 %all-gather.7.cloned.1.call-start = ((), (), s32[]{:S(2)}) async-start(), calls=%async_computation.2 | async-start | bytes 1966080 | tf_op jit(solution)/shard_map/all_gather | solution.py:108
  9.0 86.5 %all-reduce.322.cloned.1.call-start = ((), (), s32[]{:S(2)}) async-start(), calls=%async_computation.3 | async-start | bytes 4718592 | tf_op jit(solution)/shard_map/psum | solution.py:125
  39.8 145.1 %all-gather.9.cloned.1.call-start = ((), (), s32[]{:S(2)}) async-start(), calls=%async_computation.4 | async-start | bytes 1966080 | tf_op jit(solution)/shard_map/all_gather | solution.py:108
  43.4 54.2 %copy-start.553 = (f32[384]{0:T(512)}, f32[384]{0:T(512)S(1)}, u32[]{:S(2)}) copy-start(f32[384]{0:T(512)S(1)} %get-tuple-element.706) | copy-start | bytes 4612
  43.4 54.2 %copy-start.555 = (f32[384]{0:T(512)}, f32[384]{0:T(512)S(1)}, u32[]{:S(2)}) copy-start(f32[384]{0:T(512)S(1)} %get-tuple-element.707) | copy-start | bytes 4612
  100.3 27.3 %copy-start.16 = (f32[768,384]{1,0:T(8,128)}, f32[768,384]{1,0:T(8,128)S(1)}, u32[]{:S(2)}) copy-start(f32[768,384]{1,0:T(8,128)S(1)} %get-tuple-element.600) | copy-start | bytes 3538948
  100.3 27.3 %copy-start.20 = (f32[768,384]{1,0:T(8,128)}, f32[768,384]{1,0:T(8,128)S(1)}, u32[]{:S(2)}) copy-start(f32[768,384]{1,0:T(8,128)S(1)} %get-tuple-element.599) | copy-start | bytes 3538948
  106.2 21.8 %copy-start = (f32[768,384]{1,0:T(8,128)}, f32[768,384]{1,0:T(8,128)S(1)}, u32[]{:S(2)}) copy-start(f32[768,384]{1,0:T(8,128)S(1)} %get-tuple-element.376) | copy-start | bytes 3538948
  106.2 21.8 %copy-start.2 = (f32[768,384]{1,0:T(8,128)}, f32[768,384]{1,0:T(8,128)S(1)}, u32[]{:S(2)}) copy-start(f32[768,384]{1,0:T(8,128)S(1)} %get-tuple-element.377) | copy-start | bytes 3538948
  106.2 22.6 %copy-start.24 = (f32[768,384]{1,0:T(8,128)}, f32[768,384]{1,0:T(8,128)S(1)}, u32[]{:S(2)}) copy-start(f32[768,384]{1,0:T(8,128)S(1)} %get-tuple-element.375) | copy-start | bytes 3538948
  125.3 19.5 %copy-start.148 = (f32[768,384]{1,0:T(8,128)}, f32[768,384]{1,0:T(8,128)S(1)}, u32[]{:S(2)}) copy-start(f32[768,384]{1,0:T(8,128)S(1)} %get-tuple-element.382) | copy-start | bytes 3538948
  125.4 19.5 %copy-start.150 = (f32[768,384]{1,0:T(8,128)}, f32[768,384]{1,0:T(8,128)S(1)}, u32[]{:S(2)}) copy-start(f32[768,384]{1,0:T(8,128)S(1)} %get-tuple-element.383) | copy-start | bytes 3538948
  164.4 83.3 %all-reduce.324.cloned.1.call-start = ((), (), s32[]{:S(2)}) async-start(), calls=%async_computation.5 | async-start | bytes 4718592 | tf_op jit(solution)/shard_map/psum | solution.py:125
  192.0 157.6 %reduce-scatter.3.cloned.1.call-start = ((), (), s32[]{:S(2)}) async-start(), calls=%async_computation.6 | async-start | bytes 1966080 | tf_op jit(solution)/shard_map/reduce_scatter | solution.py:199
  192.1 57.7 %copy-start.557 = (f32[384]{0:T(512)}, f32[384]{0:T(512)S(1)}, u32[]{:S(2)}) copy-start(f32[384]{0:T(512)S(1)} %get-tuple-element.700) | copy-start | bytes 4612
  192.1 57.7 %copy-start.559 = (f32[384]{0:T(512)}, f32[384]{0:T(512)S(1)}, u32[]{:S(2)}) copy-start(f32[384]{0:T(512)S(1)} %get-tuple-element.701) | copy-start | bytes 4612
  253.7 27.3 %copy-start.18 = (f32[768,384]{1,0:T(8,128)}, f32[768,384]{1,0:T(8,128)S(1)}, u32[]{:S(2)}) copy-start(f32[768,384]{1,0:T(8,128)S(1)} %get-tuple-element.602) | copy-start | bytes 3538948
  253.7 27.3 %copy-start.22 = (f32[768,384]{1,0:T(8,128)}, f32[768,384]{1,0:T(8,128)S(1)}, u32[]{:S(2)}) copy-start(f32[768,384]{1,0:T(8,128)S(1)} %get-tuple-element.601) | copy-start | bytes 3538948
  259.8 21.5 %copy-start.4 = (f32[768,384]{1,0:T(8,128)}, f32[768,384]{1,0:T(8,128)S(1)}, u32[]{:S(2)}) copy-start(f32[768,384]{1,0:T(8,128)S(1)} %get-tuple-element.320) | copy-start | bytes 3538948
  259.8 21.5 %copy-start.6 = (f32[768,384]{1,0:T(8,128)}, f32[768,384]{1,0:T(8,128)S(1)}, u32[]{:S(2)}) copy-start(f32[768,384]{1,0:T(8,128)S(1)} %get-tuple-element.321) | copy-start | bytes 3538948
  259.8 22.4 %copy-start.30 = (f32[768,384]{1,0:T(8,128)}, f32[768,384]{1,0:T(8,128)S(1)}, u32[]{:S(2)}) copy-start(f32[768,384]{1,0:T(8,128)S(1)} %get-tuple-element.319) | copy-start | bytes 3538948
  278.7 19.5 %copy-start.156 = (f32[768,384]{1,0:T(8,128)}, f32[768,384]{1,0:T(8,128)S(1)}, u32[]{:S(2)}) copy-start(f32[768,384]{1,0:T(8,128)S(1)} %get-tuple-element.326) | copy-start | bytes 3538948
  278.7 19.5 %copy-start.158 = (f32[768,384]{1,0:T(8,128)}, f32[768,384]{1,0:T(8,128)S(1)}, u32[]{:S(2)}) copy-start(f32[768,384]{1,0:T(8,128)S(1)} %get-tuple-element.327) | copy-start | bytes 3538948
  320.8 130.2 %all-reduce.326.cloned.1.call-start = ((), (), s32[]{:S(2)}) async-start(), calls=%async_computation.7 | async-start | bytes 9437184 | tf_op jit(solution)/shard_map/psum | solution.py:136
  356.8 322.2 %all-gather.13.cloned.1.call-start = ((), (), s32[]{:S(2)}) async-start(), calls=%async_computation.9 | async-start | bytes 1966080 | tf_op jit(solution)/shard_map/all_gather | solution.py:118
  471.3 18.4 %copy-start.349 = (f32[768,384]{1,0:T(8,128)}, f32[768,384]{1,0:T(8,128)S(1)}, u32[]{:S(2)}) copy-start(f32[768,384]{1,0:T(8,128)S(1)} %get-tuple-element.654) | copy-start | bytes 3538948
  658.9 42.2 %all-gather.11.cloned.1.call-start = ((), (), s32[]{:S(2)}) async-start(), calls=%async_computation.8 | async-start | bytes 1966080 | tf_op jit(solution)/shard_map/all_gather | solution.py:117
  659.6 76.4 %reduce-scatter.5.cloned.1.call-start = ((), (), s32[]{:S(2)}) async-start(), calls=%async_computation.10 | async-start | bytes 1966080 | tf_op jit(solution)/shard_map/reduce_scatter | solution.py:199
  679.0 23.7 %copy-start.530 = (bf16[768,128]{1,0:T(8,128)(2,1)S(1)}, bf16[768,128]{1,0:T(8,128)(2,1)}, u32[]{:S(2)}) copy-start(bf16[768,128]{1,0:T(8,128)(2,1)} %param.20) | copy-start | bytes 589828
  680.6 22.1 %copy-start.497 = (f32[768,128]{1,0:T(8,128)S(1)}, f32[768,128]{1,0:T(8,128)}, u32[]{:S(2)}) copy-start(f32[768,128]{1,0:T(8,128)} %get-tuple-element.682) | copy-start | bytes 1179652
  680.7 22.1 %copy-start.522 = (f32[768,128]{1,0:T(8,128)S(1)}, f32[768,128]{1,0:T(8,128)}, u32[]{:S(2)}) copy-start(f32[768,128]{1,0:T(8,128)} %copy-done.521) | copy-start | bytes 1179652
  680.7 22.1 %copy-start.524 = (f32[768,128]{1,0:T(8,128)S(1)}, f32[768,128]{1,0:T(8,128)}, u32[]{:S(2)}) copy-start(f32[768,128]{1,0:T(8,128)} %copy-done.523) | copy-start | bytes 1179652
  680.7 22.1 %copy-start.525 = (f32[768,128]{1,0:T(8,128)S(1)}, f32[768,128]{1,0:T(8,128)}, u32[]{:S(2)}) copy-start(f32[768,128]{1,0:T(8,128)} %get-tuple-element.727) | copy-start | bytes 1179652
  704.6 31.4 %copy-start.498 = (f32[768,128]{1,0:T(8,128)}, f32[768,128]{1,0:T(8,128)S(1)}, u32[]{:S(2)}) copy-start(f32[768,128]{1,0:T(8,128)S(1)} %get-tuple-element.286) | copy-start | bytes 1179652
  707.7 128.3 %all-reduce.328.cloned.1.call-start = ((), (), s32[]{:S(2)}) async-start(), calls=%async_computation.11 | async-start | bytes 9437184 | tf_op jit(solution)/shard_map/psum | solution.py:136
  741.8 94.2 %copy-start.450 = (f32[256,384]{1,0:T(8,128)S(1)}, f32[256,384]{1,0:T(8,128)}, u32[]{:S(2)}) copy-start(f32[256,384]{1,0:T(8,128)} %copy-done.449) | copy-start | bytes 1179652
  741.8 94.2 %copy-start.452 = (f32[256,384]{1,0:T(8,128)S(1)}, f32[256,384]{1,0:T(8,128)}, u32[]{:S(2)}) copy-start(f32[256,384]{1,0:T(8,128)} %copy-done.451) | copy-start | bytes 1179652
  741.8 348.1 %all-gather.17.cloned.1.call-start = ((), (), s32[]{:S(2)}) async-start(), calls=%async_computation.13 | async-start | bytes 1966080 | tf_op jit(solution)/shard_map/all_gather | solution.py:118
  1035.7 55.9 %all-gather.15.cloned.1.call-start = ((), (), s32[]{:S(2)}) async-start(), calls=%async_computation.12 | async-start | bytes 1966080 | tf_op jit(solution)/shard_map/all_gather | solution.py:117
  1036.3 169.1 %all-reduce.330.cloned.1.call-start = ((), (), s32[]{:S(2)}) async-start(), calls=%async_computation.14 | async-start | bytes 5767168 | tf_op jit(solution)/shard_map/psum | solution.py:221
  1048.5 38.4 %copy-start.563 = (f32[2,3,384]{2,0,1:T(2,128)S(1)}, f32[2,3,384]{2,0,1:T(2,128)}, u32[]{:S(2)}) copy-start(f32[2,3,384]{2,0,1:T(2,128)} %param.37) | copy-start | bytes 27652
  1048.5 38.4 %copy-start.564 = (f32[2,3,384]{2,0,1:T(2,128)S(1)}, f32[2,3,384]{2,0,1:T(2,128)}, u32[]{:S(2)}) copy-start(f32[2,3,384]{2,0,1:T(2,128)} %param.32) | copy-start | bytes 27652
  1048.5 40.8 %copy-start.562 = (f32[2,4,128]{2,1,0:T(4,128)S(1)}, f32[2,4,128]{2,1,0:T(4,128)}, u32[]{:S(2)}) copy-start(f32[2,4,128]{2,1,0:T(4,128)} %param.26) | copy-start | bytes 12292
  1048.5 40.8 %copy-start.577 = (f32[2,4,128]{2,1,0:T(4,128)S(1)}, f32[2,4,128]{2,1,0:T(4,128)}, u32[]{:S(2)}) copy-start(f32[2,4,128]{2,1,0:T(4,128)} %param.36) | copy-start | bytes 12292
  1048.5 40.8 %copy-start.578 = (f32[2,4,128]{2,1,0:T(4,128)S(1)}, f32[2,4,128]{2,1,0:T(4,128)}, u32[]{:S(2)}) copy-start(f32[2,4,128]{2,1,0:T(4,128)} %param.31) | copy-start | bytes 12292
  1091.6 113.9 %copy-start.515 = (f32[2,512,128]{2,1,0:T(8,128)S(1)}, f32[2,512,128]{2,1,0:T(8,128)}, u32[]{:S(2)}) copy-start(f32[2,512,128]{2,1,0:T(8,128)} %param.25) | copy-start | bytes 1572868
  1091.6 113.9 %copy-start.547 = (f32[2,512,128]{2,1,0:T(8,128)S(1)}, f32[2,512,128]{2,1,0:T(8,128)}, u32[]{:S(2)}) copy-start(f32[2,512,128]{2,1,0:T(8,128)} %param.35) | copy-start | bytes 1572868
  1091.6 113.9 %copy-start.548 = (f32[2,512,128]{2,1,0:T(8,128)S(1)}, f32[2,512,128]{2,1,0:T(8,128)}, u32[]{:S(2)}) copy-start(f32[2,512,128]{2,1,0:T(8,128)} %param.30) | copy-start | bytes 1572868
  (557 other events, 1210.0 us)
Sparse Core Ops, SparseCore 0:
  10.2 22.5 all-gather.6
  39.9 55.6 all-reduce.321
  164.6 20.2 all-gather.8
  192.1 55.6 all-reduce.323
  320.9 28.6 reduce-scatter.2
  356.9 94.0 all-reduce.325
  659.0 19.9 all-gather.12
  681.2 19.8 all-gather.10
  707.8 28.1 reduce-scatter.4
  742.0 94.0 all-reduce.327
  1035.9 19.9 all-gather.16
  1057.9 19.8 all-gather.14
  1082.3 123.1 all-reduce.329
where the time goes:
time: 1230 us; the launch traced here: 1220 us
  waiting for transfers between devices  546 us (44%)
  other arithmetic  391 us (32%)
  local copies, waits for them, and re-layouts  167 us (14%)
  blocking collectives  53.4 us (4%)
  matrix products  42.7 us (3%)
  between operations  20.4 us (2%)
    psum x2, waiting for transfers between devices, state_backward(): states_grad = lax.psum(partial_states, 'feat')  188 us
    unnamed x1188, local copies, waits for them, and re-layouts  153 us
    neg x32, other arithmetic, combine(): mult_real = later[0] * earlier[0] - later[1] * earlier[1]  115 us
    psum x1, waiting for transfers between devices, body(): lax.psum((stacked_in, stacked_out, stacked_gate, stacked_feature, stacked...  110 us
    psum x2, waiting for transfers between devices, state_forward(): drive = lax.psum(partial_drive, 'feat')  108 us
    add_any x40, other arithmetic, combine(): add_real = later[0] * earlier[2] - later[1] * earlier[3] + later[2]  59.8 us
    neg x36, other arithmetic, combine(): add_real = later[0] * earlier[2] - later[1] * earlier[3] + later[2]  58.3 us
    reduce_scatter x2, waiting for transfers between devices, body(): lax.psum_scatter(contract_cols(pre_grad, gate_low), 'feat', scatter_dimen...  57 us
  transfers between devices with their start and end apart: 13, of which 11 were waited for; matrix products, arithmetic and copies ran while one was open for 2% of the time, Pallas kernels for 0%

commit v1 on v0

--- a/solution.py
+++ b/solution.py
@@ -10,6 +10,17 @@
 slow_rate = 0.02
 main_rate = 0.05
 weight_decay = 0.1
+
+
+def turned_line(array, name, dim):
+    devices = lax.axis_size(name)
+    route = [(i, (i + 1) % devices) for i in range(devices)]
+    parts = [array]
+    for stride in range(1, devices):
+        parts = [lax.ppermute(parts[0], name, route), *parts]
+    full = jnp.concatenate(parts, axis=dim)
+    turn = (lax.axis_index(name) + 1) * parts[-1].shape[dim]
+    return jnp.roll(full, turn, axis=dim)
 
 
 def smooth(value):
@@ -105,7 +116,7 @@
 
 
 def moments(stream):
-    whole = lax.all_gather(stream, "feat", axis=1, tiled=True)
+    whole = turned_line(stream, "feat", 1)
     center = jnp.mean(whole, 1, keepdims=True)
     spread = whole - center
     variance = jnp.mean(spread * spread, 1, keepdims=True)

time: 1230 us -> 1230 us (level)
    all_gather x2 -> x0, waiting for transfers between devices: 42.6 us -> none  [moments(): whole = lax.all_gather(stream, 'feat', axis=1, tiled=True)]
    ppermute x0 -> x6, waiting for transfers between devices: none -> 40.5 us  [turned_line(): parts = [lax.ppermute(parts[0], name, route), *parts]]
    unnamed x1188 -> x1182, local copies, waits for them, and re-layouts: 153 us -> 153 us
  transfers between devices with their start and end apart: 13 -> 17, of which waited for: 11 -> 15; matrix products, arithmetic and copies ran while one was open for 2% -> 2% of each run, Pallas kernels for 0% -> 0%
where the time goes in v1:
time: 1230 us; the launch traced here: 1220 us
  waiting for transfers between devices  547 us (44%)
  other arithmetic  390 us (32%)
  local copies, waits for them, and re-layouts  167 us (14%)
  blocking collectives  53.4 us (4%)
  matrix products  42.6 us (3%)
  between operations  20.2 us (2%)
    psum x2, waiting for transfers between devices, state_backward(): states_grad = lax.psum(partial_states, 'feat')  188 us
    unnamed x1182, local copies, waits for them, and re-layouts  153 us
    neg x32, other arithmetic, combine(): mult_real = later[0] * earlier[0] - later[1] * earlier[1]  115 us
    psum x2, waiting for transfers between devices, state_forward(): drive = lax.psum(partial_drive, 'feat')  110 us
    psum x1, waiting for transfers between devices, body(): lax.psum((stacked_in, stacked_out, stacked_gate, stacked_feature, stacked...  110 us
    add_any x40, other arithmetic, combine(): add_real = later[0] * earlier[2] - later[1] * earlier[3] + later[2]  59.9 us
    neg x36, other arithmetic, combine(): add_real = later[0] * earlier[2] - later[1] * earlier[3] + later[2]  58.3 us
    reduce_scatter x2, waiting for transfers between devices, body(): lax.psum_scatter(contract_cols(pre_grad, gate_low), 'feat', scatter_dimen...  57 us
  transfers between devices with their start and end apart: 17, of which 15 were waited for; matrix products, arithmetic and copies ran while one was open for 2% of the time, Pallas kernels for 0%

profile of v1, /device:TPU:0, one launch (start us, length us, event | category | flops | bytes accessed | tf_op | source)
XLA Modules:
  0.0 1221.5 jit_solution(9681904636097805894)
XLA Ops:
  8.7 7.4 collective-permute-done
  16.1 7.2 collective-permute-done.1
  25.8 4.7 collective-permute-done.2
  40.4 54.2 %all-reduce.322.cloned.1.call-done = f32[768,768]{1,0:T(8,128)} async-done(((f32[768,768]{1,0:T(8,128)}), f32[768,768]{1,0:T(8,128)}) %all-reduce.322.cloned.1.call-update) | async-done | bytes 2359312 | tf_op jit(solution)/shard_map/psum | solution.py:136
  153.0 8.2 all_gather.18
  163.8 6.8 collective-permute-done.3
  170.6 7.2 collective-permute-done.4
  177.8 7.2 collective-permute-done.5
  191.5 56.1 %all-reduce.324.cloned.1.call-done = f32[768,768]{1,0:T(8,128)} async-done(((f32[768,768]{1,0:T(8,128)}), f32[768,768]{1,0:T(8,128)}) %all-reduce.324.cloned.1.call-update) | async-done | bytes 2359312 | tf_op jit(solution)/shard_map/psum | solution.py:136
  306.2 8.2 all_gather.19
  320.3 28.8 %reduce-scatter.3.cloned.1.call-done = f32[768,128]{1,0:T(8,128)} async-done(((f32[768,512]{1,0:T(8,128)}), f32[768,128]{1,0:T(8,128)}) %reduce-scatter.3.cloned.1.call-update) | async-done | bytes 393232 | tf_op jit(solution)/shard_map/reduce_scatter | solution.py:210
  352.4 3.9 fusion.355
  356.7 93.7 %all-reduce.326.cloned.1.call-done = f32[768,1536]{1,0:T(8,128)} async-done(((f32[768,1536]{1,0:T(8,128)}), f32[768,1536]{1,0:T(8,128)}) %all-reduce.326.cloned.1.call-update) | async-done | bytes 4718608 | tf_op jit(solution)/shard_map/psum | solution.py:147
  450.4 5.1 fusion.496
  461.3 5.8 fusion.461
  467.2 3.6 fusion.520
  494.0 4.0 fusion.459
  505.6 3.8 fusion.458
  517.2 4.0 fusion.446
  528.3 3.9 fusion.445
  561.4 3.8 fusion.444
  573.8 3.8 fusion.443
  585.4 4.0 fusion.455
  599.1 4.0 fusion.454
  611.0 3.9 fusion.453
  621.2 3.8 multiply_reduce_fusion.3
  628.6 3.4 fusion.442
  645.1 3.5 multiply_reduce_fusion.2
  658.9 19.5 %all-gather.7.cloned.1.call-done = f32[768,512]{1,0:T(8,128)} async-done(((f32[768,128]{1,0:T(8,128)}), f32[768,512]{1,0:T(8,128)}) %all-gather.7.cloned.1.call-update) | async-done | bytes 1572880 | tf_op jit(solution)/shard_map/all_gather | solution.py:129
  680.1 20.2 %all-gather.5.cloned.1.call-done = f32[768,512]{1,0:T(8,128)} async-done(((f32[768,128]{1,0:T(8,128)}), f32[768,512]{1,0:T(8,128)}) %all-gather.5.cloned.1.call-update) | async-done | bytes 1572880 | tf_op jit(solution)/shard_map/all_gather | solution.py:128
  707.0 28.3 %reduce-scatter.5.cloned.1.call-done = f32[768,128]{1,0:T(8,128)} async-done(((f32[768,512]{1,0:T(8,128)}), f32[768,128]{1,0:T(8,128)}) %reduce-scatter.5.cloned.1.call-update) | async-done | bytes 393232 | tf_op jit(solution)/shard_map/reduce_scatter | solution.py:210
  737.2 3.9 fusion.354
  741.3 93.9 %all-reduce.328.cloned.1.call-done = f32[768,1536]{1,0:T(8,128)} async-done(((f32[768,1536]{1,0:T(8,128)}), f32[768,1536]{1,0:T(8,128)}) %all-reduce.328.cloned.1.call-update) | async-done | bytes 4718608 | tf_op jit(solution)/shard_map/psum | solution.py:147
  835.3 4.8 fusion.495
  845.8 5.0 fusion.437
  850.9 3.6 fusion.504
  894.2 3.6 fusion.422
  904.1 4.1 fusion.421
  916.0 3.8 fusion.433
  927.5 3.8 fusion.432
  939.6 3.8 fusion.420
  952.0 3.9 fusion.419
  964.0 4.0 fusion.431
  977.7 4.0 fusion.430
  989.6 3.9 fusion.429
  1006.4 3.4 fusion.418
  1049.3 37.1 %all-reduce.314 = (f32[2,4,128]{2,1,0:T(4,128)S(1)}, f32[2,3,384]{2,1,0:T(4,128)S(1)}) all-reduce(f32[2,4,128]{2,1,0:T(4,128)S(1)} %pad_maximum_fusion.10, f32[2,3,384]{2,1,0:T(4,128)S(1)} %pad_maximum_fusion.9), channel_id=1, replica_groups=mesh['seq'=8,'feat'=4] {'seq'}, use_global_device_ids=true, to_apply=%region_28.30 | all-reduce | flops 3328 | bytes 26624 | tf_op jit(solution)/shard_map/psum | solution.py:232
  1094.8 110.2 %all-reduce.330.cloned.1.call-done = (f32[2,128,768]{2,1,0:T(8,128)}, f32[2,1536,128]{2,1,0:T(8,128)}, f32[2,512,128]{2,1,0:T(8,128)}) async-done(((f32[2,128,768]{2,1,0:T(8,128)}, f32[2,1536,128]{2,1,0:T(8,128)}, f32[2,512,128]{2,1,0:T(8,128)}), (f32[2,128,768]{2,1,0:T(8,128)}, f32[2,1536,128]{2,1,0:T(8,128)}, f32[2,512,128]{2,1,0:T(8,128)})) %all-reduce.330.cloned.1.call-update) | async-done | bytes 2883600 | tf_op jit(solution)/shard_map/psum | solution.py:232
  (1613 shorter events, 482.2 us)
Async XLA Ops:
  7.2 87.5 %all-reduce.322.cloned.1.call-start = ((), (), s32[]{:S(2)}) async-start(), calls=%async_computation.2 | async-start | bytes 4718592 | tf_op jit(solution)/shard_map/psum | solution.py:136
  8.2 7.9 collective-permute-start
  16.1 7.2 collective-permute-start.1
  23.3 7.2 collective-permute-start.2
  36.8 210.8 %all-reduce.324.cloned.1.call-start = ((), (), s32[]{:S(2)}) async-start(), calls=%async_computation.3 | async-start | bytes 4718592 | tf_op jit(solution)/shard_map/psum | solution.py:136
  40.4 56.2 %copy-start.550 = (f32[384]{0:T(512)}, f32[384]{0:T(512)S(1)}, u32[]{:S(2)}) copy-start(f32[384]{0:T(512)S(1)} %get-tuple-element.711) | copy-start | bytes 4612
  40.4 56.2 %copy-start.552 = (f32[384]{0:T(512)}, f32[384]{0:T(512)S(1)}, u32[]{:S(2)}) copy-start(f32[384]{0:T(512)S(1)} %get-tuple-element.712) | copy-start | bytes 4612
  99.4 27.3 %copy-start.16 = (f32[768,384]{1,0:T(8,128)}, f32[768,384]{1,0:T(8,128)S(1)}, u32[]{:S(2)}) copy-start(f32[768,384]{1,0:T(8,128)S(1)} %get-tuple-element.605) | copy-start | bytes 3538948
  99.4 27.3 %copy-start.20 = (f32[768,384]{1,0:T(8,128)}, f32[768,384]{1,0:T(8,128)S(1)}, u32[]{:S(2)}) copy-start(f32[768,384]{1,0:T(8,128)S(1)} %get-tuple-element.604) | copy-start | bytes 3538948
  105.3 21.8 %copy-start = (f32[768,384]{1,0:T(8,128)}, f32[768,384]{1,0:T(8,128)S(1)}, u32[]{:S(2)}) copy-start(f32[768,384]{1,0:T(8,128)S(1)} %get-tuple-element.379) | copy-start | bytes 3538948
  105.3 21.8 %copy-start.2 = (f32[768,384]{1,0:T(8,128)}, f32[768,384]{1,0:T(8,128)S(1)}, u32[]{:S(2)}) copy-start(f32[768,384]{1,0:T(8,128)S(1)} %get-tuple-element.380) | copy-start | bytes 3538948
  105.3 22.6 %copy-start.24 = (f32[768,384]{1,0:T(8,128)}, f32[768,384]{1,0:T(8,128)S(1)}, u32[]{:S(2)}) copy-start(f32[768,384]{1,0:T(8,128)S(1)} %get-tuple-element.378) | copy-start | bytes 3538948
  163.4 24.9 %copy-start.399 = (f32[768,128]{1,0:T(8,128)}, f32[768,128]{1,0:T(8,128)S(1)}, u32[]{:S(2)}) copy-start(f32[768,128]{1,0:T(8,128)S(1)} %get-tuple-element.731) | copy-start | bytes 1179652
  163.4 7.3 collective-permute-start.3
  170.6 7.2 collective-permute-start.4
  177.8 7.2 collective-permute-start.5
  191.4 157.7 %reduce-scatter.3.cloned.1.call-start = ((), (), s32[]{:S(2)}) async-start(), calls=%async_computation.4 | async-start | bytes 1966080 | tf_op jit(solution)/shard_map/reduce_scatter | solution.py:210
  191.5 58.1 %copy-start.554 = (f32[384]{0:T(512)}, f32[384]{0:T(512)S(1)}, u32[]{:S(2)}) copy-start(f32[384]{0:T(512)S(1)} %get-tuple-element.705) | copy-start | bytes 4612
  191.5 58.1 %copy-start.556 = (f32[384]{0:T(512)}, f32[384]{0:T(512)S(1)}, u32[]{:S(2)}) copy-start(f32[384]{0:T(512)S(1)} %get-tuple-element.706) | copy-start | bytes 4612
  253.5 27.1 %copy-start.18 = (f32[768,384]{1,0:T(8,128)}, f32[768,384]{1,0:T(8,128)S(1)}, u32[]{:S(2)}) copy-start(f32[768,384]{1,0:T(8,128)S(1)} %get-tuple-element.607) | copy-start | bytes 3538948
  253.5 27.1 %copy-start.22 = (f32[768,384]{1,0:T(8,128)}, f32[768,384]{1,0:T(8,128)S(1)}, u32[]{:S(2)}) copy-start(f32[768,384]{1,0:T(8,128)S(1)} %get-tuple-element.606) | copy-start | bytes 3538948
  259.3 21.5 %copy-start.4 = (f32[768,384]{1,0:T(8,128)}, f32[768,384]{1,0:T(8,128)S(1)}, u32[]{:S(2)}) copy-start(f32[768,384]{1,0:T(8,128)S(1)} %get-tuple-element.321) | copy-start | bytes 3538948
  259.4 21.5 %copy-start.6 = (f32[768,384]{1,0:T(8,128)}, f32[768,384]{1,0:T(8,128)S(1)}, u32[]{:S(2)}) copy-start(f32[768,384]{1,0:T(8,128)S(1)} %get-tuple-element.322) | copy-start | bytes 3538948
  259.4 22.3 %copy-start.30 = (f32[768,384]{1,0:T(8,128)}, f32[768,384]{1,0:T(8,128)S(1)}, u32[]{:S(2)}) copy-start(f32[768,384]{1,0:T(8,128)S(1)} %get-tuple-element.320) | copy-start | bytes 3538948
  320.2 130.2 %all-reduce.326.cloned.1.call-start = ((), (), s32[]{:S(2)}) async-start(), calls=%async_computation.5 | async-start | bytes 9437184 | tf_op jit(solution)/shard_map/psum | solution.py:147
  356.3 322.1 %all-gather.7.cloned.1.call-start = ((), (), s32[]{:S(2)}) async-start(), calls=%async_computation.7 | async-start | bytes 1966080 | tf_op jit(solution)/shard_map/all_gather | solution.py:129
  658.2 42.1 %all-gather.5.cloned.1.call-start = ((), (), s32[]{:S(2)}) async-start(), calls=%async_computation.6 | async-start | bytes 1966080 | tf_op jit(solution)/shard_map/all_gather | solution.py:128
  658.8 76.5 %reduce-scatter.5.cloned.1.call-start = ((), (), s32[]{:S(2)}) async-start(), calls=%async_computation.8 | async-start | bytes 1966080 | tf_op jit(solution)/shard_map/reduce_scatter | solution.py:210
  678.4 23.5 %copy-start.527 = (bf16[768,128]{1,0:T(8,128)(2,1)S(1)}, bf16[768,128]{1,0:T(8,128)(2,1)}, u32[]{:S(2)}) copy-start(bf16[768,128]{1,0:T(8,128)(2,1)} %param.22) | copy-start | bytes 589828
  680.0 21.9 %copy-start.495 = (f32[768,128]{1,0:T(8,128)S(1)}, f32[768,128]{1,0:T(8,128)}, u32[]{:S(2)}) copy-start(f32[768,128]{1,0:T(8,128)} %get-tuple-element.687) | copy-start | bytes 1179652
  680.0 21.9 %copy-start.519 = (f32[768,128]{1,0:T(8,128)S(1)}, f32[768,128]{1,0:T(8,128)}, u32[]{:S(2)}) copy-start(f32[768,128]{1,0:T(8,128)} %copy-done.518) | copy-start | bytes 1179652
  680.1 21.9 %copy-start.521 = (f32[768,128]{1,0:T(8,128)S(1)}, f32[768,128]{1,0:T(8,128)}, u32[]{:S(2)}) copy-start(f32[768,128]{1,0:T(8,128)} %copy-done.520) | copy-start | bytes 1179652
  680.1 21.9 %copy-start.522 = (f32[768,128]{1,0:T(8,128)S(1)}, f32[768,128]{1,0:T(8,128)}, u32[]{:S(2)}) copy-start(f32[768,128]{1,0:T(8,128)} %get-tuple-element.732) | copy-start | bytes 1179652
  703.8 31.4 %copy-start.496 = (f32[768,128]{1,0:T(8,128)}, f32[768,128]{1,0:T(8,128)S(1)}, u32[]{:S(2)}) copy-start(f32[768,128]{1,0:T(8,128)S(1)} %get-tuple-element.287) | copy-start | bytes 1179652
  707.0 128.3 %all-reduce.328.cloned.1.call-start = ((), (), s32[]{:S(2)}) async-start(), calls=%async_computation.9 | async-start | bytes 9437184 | tf_op jit(solution)/shard_map/psum | solution.py:147
  741.1 94.2 %copy-start.450 = (f32[256,384]{1,0:T(8,128)S(1)}, f32[256,384]{1,0:T(8,128)}, u32[]{:S(2)}) copy-start(f32[256,384]{1,0:T(8,128)} %copy-done.449) | copy-start | bytes 1179652
  741.1 94.2 %copy-start.452 = (f32[256,384]{1,0:T(8,128)S(1)}, f32[256,384]{1,0:T(8,128)}, u32[]{:S(2)}) copy-start(f32[256,384]{1,0:T(8,128)} %copy-done.451) | copy-start | bytes 1179652
  741.1 348.3 %all-gather.11.cloned.1.call-start = ((), (), s32[]{:S(2)}) async-start(), calls=%async_computation.11 | async-start | bytes 1966080 | tf_op jit(solution)/shard_map/all_gather | solution.py:129
  1035.2 55.9 %all-gather.9.cloned.1.call-start = ((), (), s32[]{:S(2)}) async-start(), calls=%async_computation.10 | async-start | bytes 1966080 | tf_op jit(solution)/shard_map/all_gather | solution.py:128
  1035.8 169.1 %all-reduce.330.cloned.1.call-start = ((), (), s32[]{:S(2)}) async-start(), calls=%async_computation.12 | async-start | bytes 5767168 | tf_op jit(solution)/shard_map/psum | solution.py:232
  1047.9 38.4 %copy-start.560 = (f32[2,3,384]{2,0,1:T(2,128)S(1)}, f32[2,3,384]{2,0,1:T(2,128)}, u32[]{:S(2)}) copy-start(f32[2,3,384]{2,0,1:T(2,128)} %param.39) | copy-start | bytes 27652
  1047.9 38.4 %copy-start.561 = (f32[2,3,384]{2,0,1:T(2,128)S(1)}, f32[2,3,384]{2,0,1:T(2,128)}, u32[]{:S(2)}) copy-start(f32[2,3,384]{2,0,1:T(2,128)} %param.34) | copy-start | bytes 27652
  1048.0 40.9 %copy-start.559 = (f32[2,4,128]{2,1,0:T(4,128)S(1)}, f32[2,4,128]{2,1,0:T(4,128)}, u32[]{:S(2)}) copy-start(f32[2,4,128]{2,1,0:T(4,128)} %param.28) | copy-start | bytes 12292
  1048.0 40.8 %copy-start.574 = (f32[2,4,128]{2,1,0:T(4,128)S(1)}, f32[2,4,128]{2,1,0:T(4,128)}, u32[]{:S(2)}) copy-start(f32[2,4,128]{2,1,0:T(4,128)} %param.38) | copy-start | bytes 12292
  1048.0 40.8 %copy-start.575 = (f32[2,4,128]{2,1,0:T(4,128)S(1)}, f32[2,4,128]{2,1,0:T(4,128)}, u32[]{:S(2)}) copy-start(f32[2,4,128]{2,1,0:T(4,128)} %param.33) | copy-start | bytes 12292
  1091.0 113.9 %copy-start.512 = (f32[2,512,128]{2,1,0:T(8,128)S(1)}, f32[2,512,128]{2,1,0:T(8,128)}, u32[]{:S(2)}) copy-start(f32[2,512,128]{2,1,0:T(8,128)} %param.27) | copy-start | bytes 1572868
  1091.1 113.9 %copy-start.544 = (f32[2,512,128]{2,1,0:T(8,128)S(1)}, f32[2,512,128]{2,1,0:T(8,128)}, u32[]{:S(2)}) copy-start(f32[2,512,128]{2,1,0:T(8,128)} %param.37) | copy-start | bytes 1572868
  1091.1 113.9 %copy-start.545 = (f32[2,512,128]{2,1,0:T(8,128)S(1)}, f32[2,512,128]{2,1,0:T(8,128)}, u32[]{:S(2)}) copy-start(f32[2,512,128]{2,1,0:T(8,128)} %param.32) | copy-start | bytes 1572868
  (558 other events, 1311.6 us)
Sparse Core Ops, SparseCore 0:
  36.9 57.6 all-reduce.321
  191.5 56.0 all-reduce.323
  320.3 28.6 reduce-scatter.2
  356.4 94.0 all-reduce.325
  658.4 19.9 all-gather.6
  680.5 19.8 all-gather.4
  707.1 28.1 reduce-scatter.4
  741.2 94.0 all-reduce.327
  1035.4 19.9 all-gather.10
  1057.4 19.8 all-gather.8
  1081.8 123.1 all-reduce.329
